TPU v7x, 256 devices: a whole 4x4x8 slice. The times are simulated.
256 devices in a mesh: det: 64 (over x, z, core), row: 4 (over y).
Axes of the slice: x: 4, y: 4, z: 8, core: 2. Of those that a mesh axis runs over, the one named last changes fastest.
Arguments:
- images: bfloat16 [384, 3, 384, 384], P('det', None, 'row'), may hold values from -6 to 6
- warp_rows: bfloat16 [384, 3, 384, 384], P('det', None, 'row'), may hold values from -0.3125 to 0.3125
- warp_cols: bfloat16 [384, 3, 384, 384], P('det'), may hold values from -0.3125 to 0.3125
- psf_coef: float32 [384, 3, 21], P('det'), may hold values from -1.25 to 1.25
- taps: float32 [21, 21], replicated, may hold values from -1.25 to 1.25
- dest_patch: int32 [3456, 1], replicated, may hold values from 0 to 63; in each aligned block of 54 rows (0 to 53, 54 to 107, ...) at most 2 rows name the same one
- dest_block: int32 [3456], replicated, may hold values from 0 to 2
- weight_index: int32 [384, 3], replicated, may hold values from 0 to 7
- weight_table: float32 [8], replicated, may hold values from 0.25 to 4
- patch_home: int32 [64], replicated, may hold values from 0 to 63, each once
Outputs:
- difference: bfloat16 [384, 3, 384, 384], P('det', None, 'row')
- coadd: bfloat16 [64, 384, 384], P('det', 'row')
Inputs may be any that keep to these rules, and one draw needn't show every extreme that they name: `dest_patch`: within the 54 rows of one device (an aligned block of rows), no patch is named more than 2 times. `patch_home`: each position once.
All inputs are finite; a program needn't handle non-finite values.
Results may differ from a plain program's by a relative error of at most 0.0082.
Values may be sent and summed in bfloat16 or wider, within the bound.
A program may use at most 128 MiB of HBM per device.

v0:
```python
import jax
import jax.numpy as jnp
from jax import lax
from jax.sharding import PartitionSpec as P

TILE = 128


def extended(value, sides, width):
    for axis, dim in sides:
        size, length = (lax.axis_size(axis), value.shape[dim])
        up = [(i, (i + 1) % size) for i in range(size - 1)]
        down = [(j, i) for i, j in up]
        last = lax.slice_in_dim(value, length - width, length, axis=dim)
        first = lax.slice_in_dim(value, 0, width, axis=dim)
        before = lax.ppermute(last, axis, up)
        after = lax.ppermute(first, axis, down)
        value = jnp.concatenate([before, value, after], axis=dim)
    return value


def toeplitz_table(values, out_len, in_len):
    span_len = values.shape[1]
    offsets = jnp.arange(in_len)[None, :] - jnp.arange(out_len)[:, None]
    picks = (offsets[:, :, None] == jnp.arange(span_len)[None, None, :]).astype(jnp.float32)
    return jnp.einsum("oij,kj->koi", picks, values.astype(jnp.float32)).astype(jnp.bfloat16)


def per_device(
    images,
    warp_rows,
    warp_cols,
    psf_coef,
    taps,
    dest_patch,
    dest_block,
    weight_index,
    weight_table,
    patch_home,
):
    det_count, visit_count, band_rows, side_cols = images.shape
    kernel_count, tap_count = taps.shape
    reach = (tap_count - 1) // 2
    tile_cols = TILE
    tile_count = side_cols // tile_cols
    det_devices = lax.axis_size("det")
    my_index = lax.axis_index("det")
    image_count = det_count * visit_count
    piece_count = image_count * tile_count
    capacity = max(2, 2 * ((piece_count + det_devices - 1) // det_devices))
    slot_count = det_devices * capacity
    padded_rows = band_rows + 2 * reach
    col_warped = jnp.einsum(
        "dvbs,dvst->dvbt", images, warp_cols, preferred_element_type=jnp.float32
    ).astype(jnp.bfloat16)
    warped = jnp.einsum(
        "dvbr,dvrs->dvbs",
        warp_rows,
        lax.all_gather(col_warped, "row", axis=2, tiled=True),
        preferred_element_type=jnp.float32,
    ).astype(jnp.bfloat16)
    padded = extended(warped, (("row", 2),), reach)
    taps_half = taps.astype(jnp.bfloat16)
    col_table = toeplitz_table(taps_half, tile_cols, tile_cols + 2 * reach)
    tiles_in = padded.reshape(image_count, padded_rows, side_cols)
    coef_rows = psf_coef.reshape(image_count, kernel_count)

    def match_image(inputs):
        tile_image, coef_row = inputs
        widened = jnp.pad(tile_image, ((0, 0), (reach, reach)))
        windows = jnp.stack(
            [
                widened[
                    :, column_tile * tile_cols : column_tile * tile_cols + tile_cols + 2 * reach
                ]
                for column_tile in range(tile_count)
            ],
            axis=1,
        )
        conv_cols = jnp.einsum(
            "rtw,kcw->krtc", windows, col_table, preferred_element_type=jnp.float32
        ).astype(jnp.bfloat16)
        conv_cols = conv_cols.reshape(kernel_count, padded_rows, side_cols)
        scaled = (coef_row[:, None] * taps).astype(jnp.bfloat16)
        row_table = toeplitz_table(scaled, band_rows, padded_rows)
        return jnp.einsum("kbr,krs->bs", row_table, conv_cols, preferred_element_type=jnp.float32)

    matched = lax.map(match_image, (tiles_in, coef_rows))
    level_count = weight_table.shape[0]
    level_onehot = (weight_index[:, :, None] == jnp.arange(level_count)[None, None, :]).astype(
        jnp.float32
    )
    weight_all = jnp.sum(level_onehot * weight_table[None, None, :], axis=2)
    weight_mine = lax.dynamic_slice_in_dim(weight_all, my_index * det_count, det_count, 0).reshape(
        image_count
    )
    weighted = (
        (weight_mine[:, None, None] * matched)
        .astype(jnp.bfloat16)
        .reshape(image_count, band_rows, tile_count, tile_cols)
    )
    patch_count = patch_home.shape[0]
    patch_ids = dest_patch[:, 0]
    owner_all = jnp.sum(
        jnp.where(patch_ids[:, None] == jnp.arange(patch_count)[None, :], patch_home[None, :], 0),
        axis=1,
    )
    owner_grid = owner_all.reshape(det_devices, piece_count)
    earlier = jnp.arange(piece_count)[None, :] < jnp.arange(piece_count)[:, None]
    rank_grid = jnp.sum(
        ((owner_grid[:, :, None] == owner_grid[:, None, :]) & earlier[None]).astype(jnp.int32),
        axis=2,
    )
    slot_grid = owner_grid * capacity + rank_grid
    slot_mine = lax.dynamic_slice_in_dim(slot_grid, my_index, 1, 0)[0]
    send_pick = (
        (jnp.arange(slot_count)[:, None] == slot_mine[None, :])
        .astype(jnp.bfloat16)
        .reshape(slot_count, image_count, tile_count)
    )
    weight_pieces = jnp.repeat(weight_all.reshape(-1), tile_count)
    to_mine = owner_all == my_index
    block_onehot = (dest_block[:, None] == jnp.arange(tile_count)[None, :]).astype(jnp.float32)
    denominator = jnp.sum(
        jnp.where(to_mine[:, None], block_onehot * weight_pieces[:, None], 0.0), axis=0
    )
    source_slot = jnp.arange(
        det_devices * piece_count
    ) // piece_count * capacity + rank_grid.reshape(-1)
    slot_onehot = (
        (source_slot[:, None] == jnp.arange(slot_count)[None, :]) & to_mine[:, None]
    ).astype(jnp.float32)
    gather_matrix = jnp.einsum("iq,is->qs", block_onehot, slot_onehot).astype(jnp.bfloat16)
    outgoing = jnp.einsum(
        "spq,pbqc->sbc", send_pick, weighted, preferred_element_type=jnp.float32
    ).astype(jnp.bfloat16)
    received = lax.all_to_all(outgoing, "det", split_axis=0, concat_axis=0, tiled=True)
    numerator = jnp.einsum(
        "qs,sbc->bqc", gather_matrix, received, preferred_element_type=jnp.float32
    )
    template = (numerator / jnp.maximum(denominator, 1.0)[None, :, None]).astype(jnp.bfloat16)
    coadd_band = template.reshape(1, band_rows, side_cols)
    returned = jnp.einsum(
        "qs,bqc->sbc", gather_matrix, template, preferred_element_type=jnp.float32
    ).astype(jnp.bfloat16)
    arrived = lax.all_to_all(returned, "det", split_axis=0, concat_axis=0, tiled=True)
    local_template = jnp.einsum(
        "spq,sbc->pbqc", send_pick, arrived, preferred_element_type=jnp.float32
    )
    difference = (
        matched.reshape(image_count, band_rows, tile_count, tile_cols) - local_template
    ).astype(jnp.bfloat16)
    difference = difference.reshape(det_count, visit_count, band_rows, side_cols)
    return (difference, coadd_band)


def solution(mesh):
    placed = (
        P("det", None, "row", None),
        P("det", None, "row", None),
        P("det", None, None, None),
        P("det", None, None),
        P(),
        P(),
        P(),
        P(),
        P(),
        P(),
    )
    return jax.shard_map(
        per_device,
        mesh=mesh,
        in_specs=placed,
        out_specs=(P("det", None, "row", None), P("det", "row", None)),
        check_vma=False,
    )
```

profile of v0, /device:TPU:1, one launch (start us, length us, event | category | flops | bytes accessed | tf_op | source)
XLA Modules:
  0.0 490.7 jit_solution(14183806398760456192)
XLA Ops:
  8.5 4.7 convolution_convert_fusion.3
  15.2 62.1 %all-gather.2.cloned.1.call-done = bf16[6,3,384,384]{3,2,1,0:T(8,128)(2,1)} async-done(((bf16[6,3,96,384]{3,2,1,0:T(8,128)(2,1)}), bf16[6,3,384,384]{3,2,1,0:T(8,128)(2,1)}) %all-gather.2.cloned.1.call-update) | async-done | bytes 5308432 | tf_op jit(solution)/shard_map/all_gather | solution.py:59
  77.3 3.6 fusion.26
  87.8 3.8 collective-permute-done.1
  93.4 198.1 %while.12 = (s32[]{:T(128)}, f32[18,96,384]{2,1,0:T(8,128)}, f32[18,21]{1,0:T(8,128)S(1)}, f32[21,21]{1,0:T(8,128)S(1)}, bf16[18,116,384]{2,1,0:T(8,128)(2,1)}, /*index=5*/bf16[21,128,148]{1,2,0:T(8,128)(2,1)}, s32[]{:T(128)}) while((s32[]{:T(128)}, f32[18,96,384]{2,1,0:T(8,128)}, f32[18,21]{1,0:T(8,128)S(1)}, f32[21,21]{1,0:T(8,128)S(1)}, ...), condition=%wide.region_1.2_spmd, body=%wide.region_0.1_spmd.sunk | while | flops 468033056 | bytes 10274817 | solution.py:88
  95.7 3.2 convert_bitcast_fusion.2
  106.7 3.2 convert_bitcast_fusion.2
  117.7 3.2 convert_bitcast_fusion.2
  128.7 3.2 convert_bitcast_fusion.2
  139.7 3.2 convert_bitcast_fusion.2
  150.7 3.2 convert_bitcast_fusion.2
  161.7 3.2 convert_bitcast_fusion.2
  172.7 3.2 convert_bitcast_fusion.2
  183.7 3.2 convert_bitcast_fusion.2
  260.7 3.2 convert_bitcast_fusion.2
  271.7 3.2 convert_bitcast_fusion.2
  294.5 3.6 reshape.134
  300.1 3.7 copy.71
  303.8 12.1 %all-to-all-start = ((bf16[128,96,128]{2,1,0:T(8,128)(2,1)}), bf16[128,96,128]{2,1,0:T(8,128)(2,1)}, u32[]{:S(2)}, u32[]{:S(2)}) async-start(bf16[128,96,128]{2,1,0:T(8,128)(2,1)} %copy.71), calls=%async_computation | async-start | bytes 6291456 | tf_op jit(solution)/shard_map/all_to_all | solution.py:137
  318.4 71.0 %all-to-all-done = bf16[128,96,128]{2,1,0:T(8,128)(2,1)} async-done(((bf16[128,96,128]{2,1,0:T(8,128)(2,1)}), bf16[128,96,128]{2,1,0:T(8,128)(2,1)}, u32[]{:S(2)}, u32[]{:S(2)}) %all-to-all-start) | async-done | bytes 3145760 | tf_op jit(solution)/shard_map/all_to_all | solution.py:137
  393.3 3.7 copy.74
  397.0 6.2 %all-to-all-start.1 = ((bf16[128,96,128]{2,1,0:T(8,128)(2,1)}), bf16[128,96,128]{2,1,0:T(8,128)(2,1)}, u32[]{:S(2)}, u32[]{:S(2)}) async-start(bf16[128,96,128]{2,1,0:T(8,128)(2,1)} %copy.74), calls=%async_computation.1 | async-start | bytes 6291456 | tf_op jit(solution)/shard_map/all_to_all | solution.py:146
  403.9 72.7 %all-to-all-done.1 = bf16[128,96,128]{2,1,0:T(8,128)(2,1)} async-done(((bf16[128,96,128]{2,1,0:T(8,128)(2,1)}), bf16[128,96,128]{2,1,0:T(8,128)(2,1)}, u32[]{:S(2)}, u32[]{:S(2)}) %all-to-all-start.1) | async-done | bytes 3145760 | tf_op jit(solution)/shard_map/all_to_all | solution.py:146
  476.7 3.3 fusion.15
  (215 shorter events, 190.0 us)
Async XLA Ops:
  7.2 1.3 copy-start
  7.2 6.1 %copy-start.9 = (f32[8]{0:T(128)S(1)}, f32[8]{0:T(128)}, u32[]{:S(2)}) copy-start(f32[8]{0:T(128)} %param.20) | copy-start | bytes 100
  7.2 6.1 %copy-start.7 = (s32[384,3]{0,1:T(4,128)S(1)}, s32[384,3]{0,1:T(4,128)}, u32[]{:S(2)}) copy-start(s32[384,3]{0,1:T(4,128)} %param.19) | copy-start | bytes 13828
  7.2 6.4 %copy-start.6 = (f32[6,3,21]{2,1,0:T(4,128)S(1)}, f32[6,3,21]{2,1,0:T(4,128)}, u32[]{:S(2)}) copy-start(f32[6,3,21]{2,1,0:T(4,128)} %param.15) | copy-start | bytes 4540
  7.2 6.4 %copy-start.5 = (s32[3456,1]{0,1:T(1,128)S(1)}, s32[3456,1]{0,1:T(1,128)}, u32[]{:S(2)}) copy-start(s32[3456,1]{0,1:T(1,128)} %param.17) | copy-start | bytes 41476
  7.2 6.5 %copy-start.8 = (s32[64]{0:T(128)S(1)}, s32[64]{0:T(128)}, u32[]{:S(2)}) copy-start(s32[64]{0:T(128)} %param.21) | copy-start | bytes 772
  7.2 70.1 %all-gather.2.cloned.1.call-start = ((), (), s32[]{:S(2)}) async-start(), calls=%async_computation.2 | async-start | bytes 6635520 | tf_op jit(solution)/shard_map/all_gather | solution.py:59
  13.2 64.1 %copy-start.2 = (bf16[6,3,96,384]{3,2,1,0:T(8,128)(2,1)S(1)}, bf16[6,3,96,384]{3,2,1,0:T(8,128)(2,1)}, u32[]{:S(2)}) copy-start(bf16[6,3,96,384]{3,2,1,0:T(8,128)(2,1)} %param.13) | copy-start | bytes 3981316
  15.2 69.8 %copy-start.3 = (f32[21,21]{1,0:T(8,128)S(1)}, f32[21,21]{1,0:T(8,128)}, u32[]{:S(2)}) copy-start(f32[21,21]{1,0:T(8,128)} %param.16) | copy-start | bytes 5296
  81.0 6.7 %collective-permute-start = (bf16[6,3,10,384]{3,2,1,0:T(8,128)(2,1)S(1)}, bf16[6,3,10,384]{3,2,1,0:T(8,128)(2,1)S(1)}, u32[]{:S(2)}, u32[]{:S(2)}) collective-permute-start(bf16[6,3,10,384]{3,2,1,0:T(8,128)(2,1)S(1)} %get-tuple-element.125), channel_id=1, source_target_pairs={{0,1},{1,2},{2,3},{4,5},{5,6},{6,7},{8,9},{9,10},{10,11},{12,13},{... | collective-permute-start | bytes 414728 | tf_op jit(solution)/shard_map/ppermute | solution.py:16
  83.7 7.9 %collective-permute-start.1 = (bf16[6,3,10,384]{3,2,1,0:T(8,128)(2,1)S(1)}, bf16[6,3,10,384]{3,2,1,0:T(8,128)(2,1)S(1)}, u32[]{:S(2)}, u32[]{:S(2)}) collective-permute-start(bf16[6,3,10,384]{3,2,1,0:T(8,128)(2,1)S(1)} %get-tuple-element.126), channel_id=1, source_target_pairs={{1,0},{2,1},{3,2},{5,4},{6,5},{7,6},{9,8},{10,9},{11,10},{13,12},{... | collective-permute-start | bytes 414728 | tf_op jit(solution)/shard_map/ppermute | solution.py:17
  303.8 13.3 %copy-start.4 = (s32[3456]{0:T(1024)S(1)}, s32[3456]{0:T(1024)}, u32[]{:S(2)}) copy-start(s32[3456]{0:T(1024)} %param.18) | copy-start | bytes 41476
  303.8 85.6 %all-to-all-start = ((bf16[128,96,128]{2,1,0:T(8,128)(2,1)}), bf16[128,96,128]{2,1,0:T(8,128)(2,1)}, u32[]{:S(2)}, u32[]{:S(2)}) async-start(bf16[128,96,128]{2,1,0:T(8,128)(2,1)} %copy.71), calls=%async_computation | async-start | bytes 6291456 | tf_op jit(solution)/shard_map/all_to_all | solution.py:137
  397.0 79.7 %all-to-all-start.1 = ((bf16[128,96,128]{2,1,0:T(8,128)(2,1)}), bf16[128,96,128]{2,1,0:T(8,128)(2,1)}, u32[]{:S(2)}, u32[]{:S(2)}) async-start(bf16[128,96,128]{2,1,0:T(8,128)(2,1)} %copy.74), calls=%async_computation.1 | async-start | bytes 6291456 | tf_op jit(solution)/shard_map/all_to_all | solution.py:146
  476.7 3.3 copy-start.1
Sparse Core Ops, SparseCore 0:
  13.4 63.8 all-gather.1
where the time goes:
time: 495 us; the launch traced here: 491 us
  waiting for transfers between devices  211 us (43%)
  matrix products  143 us (29%)
  local copies, waits for them, and re-layouts  92.9 us (19%)
  starting transfers between devices  22.4 us (5%)
  between operations  14.4 us (3%)
  other arithmetic  7.01 us (1%)
    all_to_all x1, waiting for transfers between devices, per_device(): lax.all_to_all(returned, 'det', split_axis=0, concat_axis=0, tiled=True)  72.7 us
    all_to_all x1, waiting for transfers between devices, per_device(): lax.all_to_all(outgoing, 'det', split_axis=0, concat_axis=0, tiled=True)  71 us
    all_gather x1, waiting for transfers between devices, per_device(): lax.all_gather(col_warped, 'row', axis=2, tiled=True)  62.1 us
    dot_general x18, matrix products, match_image(): jnp.einsum('rtw,kcw->krtc', windows, col_table, preferred_element_type=jn...  57.4 us
    convert_element_type x18, local copies, waits for them, and re-layouts, match_image(): conv_cols = jnp.einsum('rtw,kcw->krtc', windows, col_table, preferred_ele...  54.3 us
    dot_general x18, matrix products, match_image(): jnp.einsum('kbr,krs->bs', row_table, conv_cols, preferred_element_type=jn...  44.7 us
    dot_general x19, matrix products, toeplitz_table(): jnp.einsum('oij,kj->koi', picks, values.astype(jnp.float32))  22.1 us
    dynamic_slice x36, local copies, waits for them, and re-layouts, per_device(): matched = lax.map(match_image, (tiles_in, coef_rows))  18.7 us
  transfers between devices with their start and end apart: 5, of which 5 were waited for; matrix products, arithmetic and copies ran while one was open for 1% of the time, Pallas kernels for 0%

commit v1 on v0

--- a/solution.py
+++ b/solution.py
@@ -56,7 +56,10 @@
     warped = jnp.einsum(
         "dvbr,dvrs->dvbs",
         warp_rows,
-        lax.all_gather(col_warped, "row", axis=2, tiled=True),
+        jnp.concatenate(
+            lax.all_to_all(jnp.stack([col_warped for _ in range(lax.psum(1, "row"))]), "row", 0, 0),
+            axis=2,
+        ),
         preferred_element_type=jnp.float32,
     ).astype(jnp.bfloat16)
     padded = extended(warped, (("row", 2),), reach)

time: 495 us -> 449 us (0.907)
  matrix products: 143 us -> 105 us
  between operations: 14.4 us -> 0.98 us
  starting transfers between devices: 22.4 us -> 32 us
  waiting for transfers between devices: 211 us -> 205 us
    all_gather x1 -> x0, waiting for transfers between devices: 62.1 us -> none  [per_device(): lax.all_gather(col_warped, 'row', axis=2, tiled=True)]
    all_to_all x0 -> x1, waiting for transfers between devices: none -> 56.6 us  [per_device(): lax.all_to_all(jnp.stack([col_warped for _ in range(lax.psum(1, 'row'))])...]
    dot_general x18, matrix products: 44.7 us -> 25.3 us  [match_image(): jnp.einsum('kbr,krs->bs', row_table, conv_cols, preferred_element_type=jn...]
    dot_general x19, matrix products: 22.1 us -> 7.15 us  [toeplitz_table(): jnp.einsum('oij,kj->koi', picks, values.astype(jnp.float32))]
    all_to_all x0 -> x1, starting transfers between devices: none -> 5.19 us  [per_device(): lax.all_to_all(jnp.stack([col_warped for _ in range(lax.psum(1, 'row'))])...]
where the time goes in v1:
time: 449 us; the launch traced here: 446 us
  waiting for transfers between devices  205 us (46%)
  matrix products  105 us (23%)
  local copies, waits for them, and re-layouts  96.2 us (21%)
  starting transfers between devices  32 us (7%)
  other arithmetic  5.93 us (1%)
    all_to_all x1, waiting for transfers between devices, per_device(): lax.all_to_all(returned, 'det', split_axis=0, concat_axis=0, tiled=True)  72.7 us
    all_to_all x1, waiting for transfers between devices, per_device(): lax.all_to_all(outgoing, 'det', split_axis=0, concat_axis=0, tiled=True)  71 us
    dot_general x18, matrix products, match_image(): jnp.einsum('rtw,kcw->krtc', windows, col_table, preferred_element_type=jn...  57.4 us
    all_to_all x1, waiting for transfers between devices, per_device(): lax.all_to_all(jnp.stack([col_warped for _ in range(lax.psum(1, 'row'))])...  56.6 us
    convert_element_type x18, local copies, waits for them, and re-layouts, match_image(): conv_cols = jnp.einsum('rtw,kcw->krtc', windows, col_table, preferred_ele...  54.3 us
    dot_general x18, matrix products, match_image(): jnp.einsum('kbr,krs->bs', row_table, conv_cols, preferred_element_type=jn...  25.3 us
    dynamic_slice x36, local copies, waits for them, and re-layouts, per_device(): matched = lax.map(match_image, (tiles_in, coef_rows))  18.5 us
    all_to_all x1, starting transfers between devices, per_device(): lax.all_to_all(outgoing, 'det', split_axis=0, concat_axis=0, tiled=True)  16.8 us
  transfers between devices with their start and end apart: 5, of which 5 were waited for; matrix products, arithmetic and copies ran while one was open for 1% of the time, Pallas kernels for 0%

profile of v1, /device:TPU:1, one launch (start us, length us, event | category | flops | bytes accessed | tf_op | source)
XLA Modules:
  0.0 445.6 jit_solution(15203651483676817325)
XLA Ops:
  2.0 3.6 convolution_convert_fusion.3
  8.6 5.2 %all-to-all-start = ((bf16[4,6,3,96,384]{4,3,2,1,0:T(8,128)(2,1)}), bf16[4,6,3,96,384]{4,3,2,1,0:T(8,128)(2,1)}, u32[]{:S(2)}, u32[]{:S(2)}) async-start(bf16[4,6,3,96,384]{4,3,2,1,0:T(8,128)(2,1)} %stack.31), calls=%async_computation | async-start | bytes 10616832 | tf_op jit(solution)/shard_map/all_to_all | solution.py:60
  16.3 56.6 %all-to-all-done = bf16[4,6,3,96,384]{4,3,2,1,0:T(8,128)(2,1)} async-done(((bf16[4,6,3,96,384]{4,3,2,1,0:T(8,128)(2,1)}), bf16[4,6,3,96,384]{4,3,2,1,0:T(8,128)(2,1)}, u32[]{:S(2)}, u32[]{:S(2)}) %all-to-all-start) | async-done | bytes 5308448 | tf_op jit(solution)/shard_map/all_to_all | solution.py:60
  72.9 3.5 copy.64
  82.9 3.8 collective-permute-done.1
  88.5 164.2 %while.12 = (s32[]{:T(128)}, f32[18,96,384]{2,1,0:T(8,128)}, f32[18,21]{1,0:T(8,128)S(1)}, f32[21,21]{1,0:T(8,128)S(1)}, bf16[18,116,384]{2,1,0:T(8,128)(2,1)}, /*index=5*/bf16[21,128,148]{1,2,0:T(8,128)(2,1)}, s32[]{:T(128)}) while((s32[]{:T(128)}, f32[18,96,384]{2,1,0:T(8,128)}, f32[18,21]{1,0:T(8,128)S(1)}, f32[21,21]{1,0:T(8,128)S(1)}, ...), condition=%wide.region_1.2_spmd, body=%wide.region_0.1_spmd.sunk | while | flops 468033056 | bytes 10153205 | solution.py:91
  89.6 3.2 convert_bitcast_fusion.2
  98.7 3.2 convert_bitcast_fusion.2
  126.1 3.2 convert_bitcast_fusion.2
  135.2 3.2 convert_bitcast_fusion.2
  144.3 3.2 convert_bitcast_fusion.2
  162.6 3.2 convert_bitcast_fusion.2
  171.7 3.2 convert_bitcast_fusion.2
  189.9 3.2 convert_bitcast_fusion.2
  199.0 3.2 convert_bitcast_fusion.2
  208.2 3.2 convert_bitcast_fusion.2
  217.3 3.2 convert_bitcast_fusion.2
  257.1 3.7 copy.74
  260.8 16.8 %all-to-all-start.1 = ((bf16[128,96,128]{2,1,0:T(8,128)(2,1)}), bf16[128,96,128]{2,1,0:T(8,128)(2,1)}, u32[]{:S(2)}, u32[]{:S(2)}) async-start(bf16[128,96,128]{2,1,0:T(8,128)(2,1)} %copy.74), calls=%async_computation.1 | async-start | bytes 6291456 | tf_op jit(solution)/shard_map/all_to_all | solution.py:140
  280.1 71.0 %all-to-all-done.1 = bf16[128,96,128]{2,1,0:T(8,128)(2,1)} async-done(((bf16[128,96,128]{2,1,0:T(8,128)(2,1)}), bf16[128,96,128]{2,1,0:T(8,128)(2,1)}, u32[]{:S(2)}, u32[]{:S(2)}) %all-to-all-start.1) | async-done | bytes 3145760 | tf_op jit(solution)/shard_map/all_to_all | solution.py:140
  355.0 3.7 copy.77
  358.7 6.2 %all-to-all-start.2 = ((bf16[128,96,128]{2,1,0:T(8,128)(2,1)}), bf16[128,96,128]{2,1,0:T(8,128)(2,1)}, u32[]{:S(2)}, u32[]{:S(2)}) async-start(bf16[128,96,128]{2,1,0:T(8,128)(2,1)} %copy.77), calls=%async_computation.2 | async-start | bytes 6291456 | tf_op jit(solution)/shard_map/all_to_all | solution.py:149
  365.6 72.7 %all-to-all-done.2 = bf16[128,96,128]{2,1,0:T(8,128)(2,1)} async-done(((bf16[128,96,128]{2,1,0:T(8,128)(2,1)}), bf16[128,96,128]{2,1,0:T(8,128)(2,1)}, u32[]{:S(2)}, u32[]{:S(2)}) %all-to-all-start.2) | async-done | bytes 3145760 | tf_op jit(solution)/shard_map/all_to_all | solution.py:149
  438.4 3.3 fusion.15
  (218 shorter events, 158.4 us)
Async XLA Ops:
  0.6 1.3 copy-start
  8.6 5.3 %copy-start.8 = (s32[384,3]{0,1:T(4,128)S(1)}, s32[384,3]{0,1:T(4,128)}, u32[]{:S(2)}) copy-start(s32[384,3]{0,1:T(4,128)} %param.19) | copy-start | bytes 13828
  8.6 5.3 %copy-start.10 = (f32[8]{0:T(128)S(1)}, f32[8]{0:T(128)}, u32[]{:S(2)}) copy-start(f32[8]{0:T(128)} %param.20) | copy-start | bytes 100
  8.6 5.6 %copy-start.4 = (f32[21,21]{1,0:T(8,128)S(1)}, f32[21,21]{1,0:T(8,128)}, u32[]{:S(2)}) copy-start(f32[21,21]{1,0:T(8,128)} %param.16) | copy-start | bytes 5296
  8.6 64.3 %all-to-all-start = ((bf16[4,6,3,96,384]{4,3,2,1,0:T(8,128)(2,1)}), bf16[4,6,3,96,384]{4,3,2,1,0:T(8,128)(2,1)}, u32[]{:S(2)}, u32[]{:S(2)}) async-start(bf16[4,6,3,96,384]{4,3,2,1,0:T(8,128)(2,1)} %stack.31), calls=%async_computation | async-start | bytes 10616832 | tf_op jit(solution)/shard_map/all_to_all | solution.py:60
  13.8 2.0 copy-start.7
  13.8 2.0 copy-start.6
  13.8 2.0 copy-start.9
  72.9 3.5 copy-start.3
  77.6 5.3 %collective-permute-start = (bf16[6,3,10,384]{3,2,1,0:T(8,128)(2,1)S(1)}, bf16[6,3,10,384]{3,2,1,0:T(8,128)(2,1)S(1)}, u32[]{:S(2)}, u32[]{:S(2)}) collective-permute-start(bf16[6,3,10,384]{3,2,1,0:T(8,128)(2,1)S(1)} %get-tuple-element.125), channel_id=1, source_target_pairs={{0,1},{1,2},{2,3},{4,5},{5,6},{6,7},{8,9},{9,10},{10,11},{12,13},{... | collective-permute-start | bytes 414728 | tf_op jit(solution)/shard_map/ppermute | solution.py:16
  80.0 6.7 %collective-permute-start.1 = (bf16[6,3,10,384]{3,2,1,0:T(8,128)(2,1)S(1)}, bf16[6,3,10,384]{3,2,1,0:T(8,128)(2,1)S(1)}, u32[]{:S(2)}, u32[]{:S(2)}) collective-permute-start(bf16[6,3,10,384]{3,2,1,0:T(8,128)(2,1)S(1)} %get-tuple-element.126), channel_id=1, source_target_pairs={{1,0},{2,1},{3,2},{5,4},{6,5},{7,6},{9,8},{10,9},{11,10},{13,12},{... | collective-permute-start | bytes 414728 | tf_op jit(solution)/shard_map/ppermute | solution.py:17
  260.8 18.0 %copy-start.5 = (s32[3456]{0:T(1024)S(1)}, s32[3456]{0:T(1024)}, u32[]{:S(2)}) copy-start(s32[3456]{0:T(1024)} %param.18) | copy-start | bytes 41476
  260.8 90.3 %all-to-all-start.1 = ((bf16[128,96,128]{2,1,0:T(8,128)(2,1)}), bf16[128,96,128]{2,1,0:T(8,128)(2,1)}, u32[]{:S(2)}, u32[]{:S(2)}) async-start(bf16[128,96,128]{2,1,0:T(8,128)(2,1)} %copy.74), calls=%async_computation.1 | async-start | bytes 6291456 | tf_op jit(solution)/shard_map/all_to_all | solution.py:140
  358.7 79.7 %all-to-all-start.2 = ((bf16[128,96,128]{2,1,0:T(8,128)(2,1)}), bf16[128,96,128]{2,1,0:T(8,128)(2,1)}, u32[]{:S(2)}, u32[]{:S(2)}) async-start(bf16[128,96,128]{2,1,0:T(8,128)(2,1)} %copy.77), calls=%async_computation.2 | async-start | bytes 6291456 | tf_op jit(solution)/shard_map/all_to_all | solution.py:149
  438.4 3.3 copy-start.2
  441.7 3.9 copy-start.1
